TPU v7x, 32 devices: a whole 2x2x4 slice. The times are simulated.
32 devices in a mesh: fx: 2 (over y), fy: 4 (over x, core), st: 4 (over z).
Axes of the slice: x: 2, y: 2, z: 4, core: 2. Of those that a mesh axis runs over, the one named last changes fastest.
Arguments:
- tangent_rhs: bfloat16 [4, 6, 64, 2, 4, 128], P('st', None, None, 'fx', 'fy'), may hold values from -6 to 6
- adjoint_rhs: bfloat16 [4, 6, 64, 2, 4, 128], P('st', None, None, 'fx', 'fy'), may hold values from -6 to 6
- jacobians: bfloat16 [3, 6, 6, 2, 4, 128], P(None, None, None, 'fx', 'fy'), may hold values from -0.75 to 0.75
- deriv: bfloat16 [3, 64, 64], replicated, may hold values from -0.75 to 0.75
- penalty: float32 [6], replicated, may hold values from 0.1 to 0.4
- second_order: float32 [6, 2, 4, 128], P(None, 'fx', 'fy'), may hold values from -4 to 4
- coupling: bfloat16 [6, 384], replicated, may hold values from -2.5 to 2.5
- shell_inverse: bfloat16 [16, 384, 384], P('st')
- shell_load: float32 [4, 16, 384], P(None, 'st'), may hold values from -6 to 6
- shell_adjoint_rhs: float32 [4, 16, 384], P(None, 'st'), may hold values from -6 to 6
- iface_elem: int32 [8, 128], P(('fx', 'fy')), may hold values from 0 to 127
- iface_node: int32 [8, 128], P(('fx', 'fy')), may hold values from 0 to 1023
- iface_weight: float32 [8, 128], P(('fx', 'fy')), may hold values from 0.5 to 2
- iface_count: int32 [8], P(('fx', 'fy')), may hold values from 0 to 128, as said below
Outputs:
- tangent_flow: bfloat16 [4, 6, 64, 2, 4, 128], P('st', None, None, 'fx', 'fy')
- adjoint_flow: bfloat16 [4, 6, 64, 2, 4, 128], P('st', None, None, 'fx', 'fy')
- shell_tangent: float32 [4, 16, 384], P(None, 'st')
- shell_adjoint: float32 [4, 16, 384], P(None, 'st')
Inputs may be any that keep to these rules, and one draw needn't show every extreme that they name: `iface_count`: at most 128 live slots in one flow block; some block has exactly 128.
All inputs are finite; a program needn't handle non-finite values.
Results may differ from a plain program's by a relative error of at most 0.0069.
Values may be sent and summed in bfloat16 or wider, within the bound.
No kernel may reach another device: no remote copies, remote signals or barrier semaphores. Data moves between devices by JAX's collectives and lax.ppermute only.
A program may use at most 64 MiB of HBM per device.

v0:
```python
import jax
import jax.numpy as jnp
from jax import lax
from jax.sharding import PartitionSpec as P

SDOF = 6
PN = 64
FSWEEP = 3
ROUNDS = 2
SIGMA = 0.5


def with_halo(value, sides, width):
    for axis, dim in sides:
        peers, length = (lax.axis_size(axis), value.shape[dim])
        up = [(i, (i + 1) % peers) for i in range(peers - 1)]
        down = [(j, i) for i, j in up]
        last = lax.slice_in_dim(value, length - width, length, axis=dim)
        initial = lax.slice_in_dim(value, 0, width, axis=dim)
        before = lax.ppermute(last, axis, up)
        after = lax.ppermute(initial, axis, down)
        value = jnp.concatenate([before, value, after], axis=dim)
    return value


def face_pair(lower_face, upper_face, below, above, axis):
    length = lower_face.shape[axis]
    beyond_upper = jnp.concatenate(
        [lax.slice_in_dim(lower_face, 1, length, axis=axis), above], axis=axis
    )
    beyond_lower = jnp.concatenate(
        [below, lax.slice_in_dim(upper_face, 0, length - 1, axis=axis)], axis=axis
    )
    return (lower_face - beyond_lower, upper_face - beyond_upper)


def place_faces(jump_low, jump_high, axis):
    middle_shape = list(jump_low.shape)
    middle_shape.insert(axis, 2)
    middle = jnp.zeros(middle_shape, jump_low.dtype)
    return jnp.concatenate(
        [jnp.expand_dims(jump_low, axis), middle, jnp.expand_dims(jump_high, axis)], axis=axis
    )


def as_cube(values):
    members, variables, points, size_x, size_y, size_z = values.shape
    return values.reshape(members, variables, 4, 4, 4, size_x, size_y, size_z)


def face_edges(values):
    cube = as_cube(values)
    received = []
    for node_axis in (2, 3):
        elem_axis = node_axis + 2
        lower_face = jnp.take(cube, 0, axis=node_axis)
        upper_face = jnp.take(cube, 3, axis=node_axis)
        edges = jnp.concatenate([lower_face, upper_face], axis=elem_axis)
        if node_axis == 2:
            extended = with_halo(edges, (("fx", 4),), 1)
        else:
            extended = with_halo(edges, (("fy", 5),), 1)
        below = lax.slice_in_dim(extended, 0, 1, axis=elem_axis)
        above = lax.slice_in_dim(extended, 3, 4, axis=elem_axis)
        received.append((below, above))
    return received


def flow_jumps(values, received):
    cube = as_cube(values)
    result = jnp.zeros(cube.shape, jnp.float32)
    for node_axis in (2, 3, 4):
        elem_axis = node_axis + 2
        lower_face = jnp.take(cube, 0, axis=node_axis).astype(jnp.float32)
        upper_face = jnp.take(cube, 3, axis=node_axis).astype(jnp.float32)
        if received is None or node_axis == 4:
            below = jnp.zeros_like(lax.slice_in_dim(lower_face, 0, 1, axis=elem_axis))
            above = below
        else:
            below = received[node_axis - 2][0].astype(jnp.float32)
            above = received[node_axis - 2][1].astype(jnp.float32)
        jump_low, jump_high = face_pair(lower_face, upper_face, below, above, elem_axis)
        result = result + place_faces(jump_low, jump_high, node_axis)
    return result.reshape(values.shape)


def volume(values, deriv_mats, jac_mats):
    grads = jnp.einsum("kpq,vqxyz->kvpxyz", deriv_mats, values, preferred_element_type=jnp.float32)
    result = jnp.sum(jac_mats[0][:, :, None] * grads[0][None], axis=1)
    for axis_index in (1, 2):
        result = result + jnp.sum(
            jac_mats[axis_index][:, :, None] * grads[axis_index][None], axis=1
        )
    return result


def operator(states, operator_kinds, penalty):
    values = lax.optimization_barrier(states.astype(jnp.bfloat16))
    received = face_edges(values)
    jumps = flow_jumps(values, received)
    volumes = jnp.stack(
        [
            volume(values[member], operator_kinds[member][0], operator_kinds[member][1])
            for member in range(len(operator_kinds))
        ]
    )
    return states + volumes + penalty[None, :, None, None, None, None] * jumps


def body(
    tangent_rhs,
    adjoint_rhs,
    jacobians,
    deriv,
    penalty,
    second_order,
    coupling,
    shell_inverse,
    shell_load,
    shell_adjoint_rhs,
    iface_elem,
    iface_node,
    iface_weight,
    iface_count,
):
    state_shape = tangent_rhs.shape
    variables = state_shape[1]
    points = state_shape[2]
    elements = state_shape[3] * state_shape[4] * state_shape[5]
    slots = iface_elem.shape[1]
    live = (jnp.arange(slots, dtype=jnp.int32) < iface_count[0]).astype(jnp.float32)
    weights = iface_weight[0] * live
    elem_index = iface_elem[0]
    node_index = iface_node[0]
    dof_rows = jnp.arange(SDOF, dtype=jnp.int32)[:, None]
    columns = (node_index // PN)[None, :] * (SDOF * PN) + dof_rows * PN + (node_index % PN)[None, :]
    forward_jac = jacobians.astype(jnp.float32)
    forward_kind = (deriv, forward_jac)
    backward_kind = (jnp.swapaxes(deriv, 1, 2), jnp.swapaxes(forward_jac, 1, 2))
    coupling_cols = coupling.T

    def shell_solve(rhs):
        return jnp.einsum(
            "pab,dpb->dpa",
            shell_inverse,
            rhs.astype(jnp.bfloat16),
            preferred_element_type=jnp.float32,
        )

    shell_tangent = shell_solve(shell_load)
    shell_adjoint = jnp.zeros(shell_load.shape, jnp.float32)
    tangent = jnp.zeros(state_shape, jnp.float32)
    adjoint = jnp.zeros(state_shape, jnp.float32)
    for round_index in range(ROUNDS):
        received = lax.all_to_all(
            shell_tangent.astype(jnp.bfloat16), "st", split_axis=0, concat_axis=1, tiled=True
        )
        picked = received.reshape(-1)[columns]
        pushed_cols = (
            jnp.dot(coupling_cols, picked, preferred_element_type=jnp.float32) * weights[None, :]
        )
        pushed = (
            jnp.zeros((variables * points, elements), jnp.float32)
            .at[:, elem_index]
            .add(pushed_cols)
        )
        force = tangent_rhs.astype(jnp.float32) - pushed.reshape(state_shape)
        adjoint_source = adjoint_rhs.astype(jnp.float32) + second_order[None, :, None] * tangent
        paired = jnp.concatenate([tangent, adjoint])
        sources = jnp.concatenate([force, adjoint_source])
        for sweep in range(FSWEEP):
            paired = paired + SIGMA * (
                sources - operator(paired, (forward_kind, backward_kind), penalty)
            )
        tangent = paired[:1]
        adjoint = paired[1:]
        adjoint_values = adjoint.astype(jnp.bfloat16).reshape(variables * points, elements)
        gathered = adjoint_values[:, elem_index]
        loads = jnp.dot(coupling, gathered, preferred_element_type=jnp.float32) * weights[None, :]
        panels = received.shape[1]
        partial_loads = jnp.zeros((panels * SDOF * PN,), jnp.float32).at[columns].add(loads)
        partial_loads = partial_loads.reshape(1, panels, SDOF * PN)
        summed = lax.psum(partial_loads, ("fx", "fy"))
        owned = lax.all_to_all(summed, "st", split_axis=1, concat_axis=0, tiled=True)
        shell_adjoint = shell_solve(shell_adjoint_rhs - owned)
        shell_tangent = shell_solve(shell_load + shell_adjoint)
    return (
        tangent.astype(jnp.bfloat16),
        adjoint.astype(jnp.bfloat16),
        shell_tangent,
        shell_adjoint,
    )


def solution(mesh):
    in_specs = (
        P("st", None, None, "fx", "fy", None),
        P("st", None, None, "fx", "fy", None),
        P(None, None, None, "fx", "fy", None),
        P(),
        P(),
        P(None, "fx", "fy", None),
        P(),
        P("st", None, None),
        P(None, "st", None),
        P(None, "st", None),
        P(("fx", "fy"), None),
        P(("fx", "fy"), None),
        P(("fx", "fy"), None),
        P(("fx", "fy")),
    )
    out_specs = (
        P("st", None, None, "fx", "fy", None),
        P("st", None, None, "fx", "fy", None),
        P(None, "st", None),
        P(None, "st", None),
    )
    return jax.shard_map(body, mesh=mesh, in_specs=in_specs, out_specs=out_specs, check_vma=False)
```

profile of v0, /device:TPU:0, one launch (start us, length us, event | category | flops | bytes accessed | tf_op | source)
XLA Modules:
  0.0 207.5 jit_solution(6584082621477791752)
XLA Ops:
  0.7 5.0 %collective-permute-start = (bf16[2,6,4,4,1,1,128]{6,3,2,1,0,5,4:T(4,128)(2,1)S(1)}, bf16[2,6,4,4,1,1,128]{6,3,2,1,0,5,4:T(4,128)(2,1)S(1)}, u32[]{:S(2)}, u32[]{:S(2)}) collective-permute-start(bf16[2,6,4,4,1,1,128]{6,3,2,1,0,5,4:T(4,128)(2,1)S(1)} %get-tuple-element.197), channel_id=1, source_target_pairs={{0,16},{1,17},{2,18},{3,19},{4,20},{5,21},{6,22},{7,23},{8,24},{9,... | collective-permute-start | bytes 147464 | tf_op jit(solution)/shard_map/ppermute | solution.py:20
  11.7 4.9 %all-to-all-start = ((bf16[4,4,384]{2,1,0:T(4,128)(2,1)}), bf16[4,4,384]{2,1,0:T(4,128)(2,1)S(1)}, u32[]{:S(2)}, u32[]{:S(2)}) async-start(bf16[4,4,384]{2,1,0:T(4,128)(2,1)} %copy.260), calls=%async_computation | async-start | bytes 24576 | tf_op jit(solution)/shard_map/all_to_all | solution.py:155
  22.2 5.0 %gather_fusion = bf16[768]{0:T(1024)(128)(2,1)S(1)} fusion(bf16[6144]{0:T(1024)(128)(2,1)S(1)} %reshape.2599, s32[1024]{0:T(1024)S(1)} %pad_clamp_fusion.1), kind=kCustom, calls=%fused_computation | custom fusion | bytes 6144 | tf_op jit(solution)/shard_map/gather | solution.py:158
  31.5 4.4 %collective-permute-start.4 = (bf16[2,6,4,4,1,1,128]{6,3,2,1,0,5,4:T(4,128)(2,1)S(1)}, bf16[2,6,4,4,1,1,128]{6,3,2,1,0,5,4:T(4,128)(2,1)S(1)}, u32[]{:S(2)}, u32[]{:S(2)}) collective-permute-start(bf16[2,6,4,4,1,1,128]{6,3,2,1,0,5,4:T(4,128)(2,1)S(1)} %get-tuple-element.187), channel_id=1, source_target_pairs={{0,16},{1,17},{2,18},{3,19},{4,20},{5,21},{6,22},{7,23},{8,24},{9,... | collective-permute-start | bytes 147464 | tf_op jit(solution)/shard_map/ppermute | solution.py:20
  37.2 3.0 %collective-permute-start.6 = (bf16[2,6,4,4,1,1,128]{6,3,2,1,0,5,4:T(4,128)(2,1)S(1)}, bf16[2,6,4,4,1,1,128]{6,3,2,1,0,5,4:T(4,128)(2,1)S(1)}, u32[]{:S(2)}, u32[]{:S(2)}) collective-permute-start(bf16[2,6,4,4,1,1,128]{6,3,2,1,0,5,4:T(4,128)(2,1)S(1)} %get-tuple-element.185), channel_id=1, source_target_pairs={{0,4},{4,8},{8,12},{1,5},{5,9},{9,13},{2,6},{6,10},{10,14},{3,7},{... | collective-permute-start | bytes 147464 | tf_op jit(solution)/shard_map/ppermute | solution.py:20
  42.3 4.1 %collective-permute-done.7 = bf16[2,6,4,4,1,1,128]{6,3,2,1,0,5,4:T(4,128)(2,1)S(1)} collective-permute-done((bf16[2,6,4,4,1,1,128]{6,3,2,1,0,5,4:T(4,128)(2,1)S(1)}, bf16[2,6,4,4,1,1,128]{6,3,2,1,0,5,4:T(4,128)(2,1)S(1)}, u32[]{:S(2)}, u32[]{:S(2)}) %collective-permute-start.7) | collective-permute-done | bytes 49184 | tf_op jit(solution)/shard_map/ppermute | solution.py:21
  48.7 4.7 %collective-permute-start.10 = (bf16[2,6,4,4,1,1,128]{6,3,2,1,0,5,4:T(4,128)(2,1)S(1)}, bf16[2,6,4,4,1,1,128]{6,3,2,1,0,5,4:T(4,128)(2,1)S(1)}, u32[]{:S(2)}, u32[]{:S(2)}) collective-permute-start(bf16[2,6,4,4,1,1,128]{6,3,2,1,0,5,4:T(4,128)(2,1)S(1)} %get-tuple-element.175), channel_id=1, source_target_pairs={{0,4},{4,8},{8,12},{1,5},{5,9},{9,13},{2,6},{6,10},{10,14},{3,7},{... | collective-permute-start | bytes 147464 | tf_op jit(solution)/shard_map/ppermute | solution.py:20
  54.7 4.5 %collective-permute-start.8 = (bf16[2,6,4,4,1,1,128]{6,3,2,1,0,5,4:T(4,128)(2,1)S(1)}, bf16[2,6,4,4,1,1,128]{6,3,2,1,0,5,4:T(4,128)(2,1)S(1)}, u32[]{:S(2)}, u32[]{:S(2)}) collective-permute-start(bf16[2,6,4,4,1,1,128]{6,3,2,1,0,5,4:T(4,128)(2,1)S(1)} %get-tuple-element.177), channel_id=1, source_target_pairs={{0,16},{1,17},{2,18},{3,19},{4,20},{5,21},{6,22},{7,23},{8,24},{9,... | collective-permute-start | bytes 147464 | tf_op jit(solution)/shard_map/ppermute | solution.py:20
  61.2 4.4 %collective-permute-done.9 = bf16[2,6,4,4,1,1,128]{6,3,2,1,0,5,4:T(4,128)(2,1)S(1)} collective-permute-done((bf16[2,6,4,4,1,1,128]{6,3,2,1,0,5,4:T(4,128)(2,1)S(1)}, bf16[2,6,4,4,1,1,128]{6,3,2,1,0,5,4:T(4,128)(2,1)S(1)}, u32[]{:S(2)}, u32[]{:S(2)}) %collective-permute-start.9) | collective-permute-done | bytes 49184 | tf_op jit(solution)/shard_map/ppermute | solution.py:21
  71.2 2.1 collective-permute-start.12
  75.3 4.8 %scatter_custom_fusion.1 = f32[6144]{0:T(1024)S(1)} fusion(s32[768]{0:T(1024)} %copy-done.12, f32[768]{0:T(1024)S(1)} %fusion.5, f32[]{:T(128)} %constant.129.clone.1), kind=kCustom, calls=%fused_computation.296 | custom fusion | flops 768 | bytes 25088 | tf_op jit(solution)/shard_map/scatter-add | solution.py:181
  80.0 23.1 %psum.14 = f32[1,16,384]{2,0,1:T(1,128)} all-reduce(f32[1,16,384]{2,0,1:T(1,128)S(1)} %bitcast.739), channel_id=1, replica_groups=mesh['fx'=2,'fy'=4,'st'=4] {'fx','fy'}, use_global_device_ids=true, to_apply=%region_20.27 | all-reduce | flops 6144 | bytes 49152 | tf_op jit(solution)/shard_map/psum | solution.py:183
  103.2 3.9 %all-to-all-start.1 = ((f32[1,16,384]{2,0,1:T(1,128)}), f32[1,16,384]{2,0,1:T(1,128)}, u32[]{:S(2)}, u32[]{:S(2)}) async-start(f32[1,16,384]{2,0,1:T(1,128)} %psum.14), calls=%async_computation.1 | async-start | bytes 49152 | tf_op jit(solution)/shard_map/all_to_all | solution.py:184
  117.6 5.1 %all-to-all-start.2 = ((bf16[4,4,384]{2,1,0:T(4,128)(2,1)}), bf16[4,4,384]{2,1,0:T(4,128)(2,1)S(1)}, u32[]{:S(2)}, u32[]{:S(2)}) async-start(bf16[4,4,384]{2,1,0:T(4,128)(2,1)} %copy.301), calls=%async_computation.2 | async-start | bytes 24576 | tf_op jit(solution)/shard_map/all_to_all | solution.py:155
  123.9 4.4 %all-to-all-done.2 = bf16[4,4,384]{2,1,0:T(4,128)(2,1)S(1)} async-done(((bf16[4,4,384]{2,1,0:T(4,128)(2,1)}), bf16[4,4,384]{2,1,0:T(4,128)(2,1)S(1)}, u32[]{:S(2)}, u32[]{:S(2)}) %all-to-all-start.2) | async-done | bytes 12320 | tf_op jit(solution)/shard_map/all_to_all | solution.py:155
  128.3 5.0 %gather_fusion.2 = bf16[768]{0:T(1024)(128)(2,1)S(1)} fusion(bf16[6144]{0:T(1024)(128)(2,1)S(1)} %reshape.2612, s32[1024]{0:T(1024)S(1)} %pad_clamp_fusion.1), kind=kCustom, calls=%fused_computation.2 | custom fusion | bytes 6144 | tf_op jit(solution)/shard_map/gather | solution.py:158
  137.1 4.5 %collective-permute-start.16 = (bf16[2,6,4,4,1,1,128]{6,3,2,1,0,5,4:T(4,128)(2,1)S(1)}, bf16[2,6,4,4,1,1,128]{6,3,2,1,0,5,4:T(4,128)(2,1)S(1)}, u32[]{:S(2)}, u32[]{:S(2)}) collective-permute-start(bf16[2,6,4,4,1,1,128]{6,3,2,1,0,5,4:T(4,128)(2,1)S(1)} %get-tuple-element.157), channel_id=1, source_target_pairs={{0,16},{1,17},{2,18},{3,19},{4,20},{5,21},{6,22},{7,23},{8,24},{9,... | collective-permute-start | bytes 147464 | tf_op jit(solution)/shard_map/ppermute | solution.py:20
  145.7 1.9 collective-permute-done.17
  147.6 1.9 collective-permute-done.19
  151.2 4.5 %collective-permute-start.20 = (bf16[2,6,4,4,1,1,128]{6,3,2,1,0,5,4:T(4,128)(2,1)S(1)}, bf16[2,6,4,4,1,1,128]{6,3,2,1,0,5,4:T(4,128)(2,1)S(1)}, u32[]{:S(2)}, u32[]{:S(2)}) collective-permute-start(bf16[2,6,4,4,1,1,128]{6,3,2,1,0,5,4:T(4,128)(2,1)S(1)} %get-tuple-element.147), channel_id=1, source_target_pairs={{0,16},{1,17},{2,18},{3,19},{4,20},{5,21},{6,22},{7,23},{8,24},{9,... | collective-permute-start | bytes 147464 | tf_op jit(solution)/shard_map/ppermute | solution.py:20
  157.0 4.4 %collective-permute-start.22 = (bf16[2,6,4,4,1,1,128]{6,3,2,1,0,5,4:T(4,128)(2,1)S(1)}, bf16[2,6,4,4,1,1,128]{6,3,2,1,0,5,4:T(4,128)(2,1)S(1)}, u32[]{:S(2)}, u32[]{:S(2)}) collective-permute-start(bf16[2,6,4,4,1,1,128]{6,3,2,1,0,5,4:T(4,128)(2,1)S(1)} %get-tuple-element.145), channel_id=1, source_target_pairs={{0,4},{4,8},{8,12},{1,5},{5,9},{9,13},{2,6},{6,10},{10,14},{3,7},{... | collective-permute-start | bytes 147464 | tf_op jit(solution)/shard_map/ppermute | solution.py:20
  167.3 4.8 %scatter_custom_fusion.3 = f32[6144]{0:T(1024)S(1)} fusion(s32[768]{0:T(1024)} %copy-done.12, f32[768]{0:T(1024)S(1)} %fusion.4, f32[]{:T(128)} %constant.129.clone.1), kind=kCustom, calls=%fused_computation.294 | custom fusion | flops 768 | bytes 25088 | tf_op jit(solution)/shard_map/scatter-add | solution.py:181
  172.0 25.3 %psum.15 = f32[1,16,384]{2,0,1:T(1,128)S(1)} all-reduce(f32[1,16,384]{2,0,1:T(1,128)S(1)} %bitcast.738), channel_id=1, replica_groups=mesh['fx'=2,'fy'=4,'st'=4] {'fx','fy'}, use_global_device_ids=true, to_apply=%region_41.48 | all-reduce | flops 6144 | bytes 49152 | tf_op jit(solution)/shard_map/psum | solution.py:183
  197.3 8.0 %all_to_all.42 = f32[1,16,384]{2,0,1:T(1,128)S(1)} all-to-all(f32[1,16,384]{2,0,1:T(1,128)S(1)} %psum.15), channel_id=1, replica_groups=mesh['fx'=2,'fy'=4,'st'=4] {'st'}, dimensions={1} | all-to-all | bytes 49152 | tf_op jit(solution)/shard_map/all_to_all | solution.py:184
  (264 shorter events, 60.9 us)
Async XLA Ops:
  0.7 28.4 %collective-permute-start = (bf16[2,6,4,4,1,1,128]{6,3,2,1,0,5,4:T(4,128)(2,1)S(1)}, bf16[2,6,4,4,1,1,128]{6,3,2,1,0,5,4:T(4,128)(2,1)S(1)}, u32[]{:S(2)}, u32[]{:S(2)}) collective-permute-start(bf16[2,6,4,4,1,1,128]{6,3,2,1,0,5,4:T(4,128)(2,1)S(1)} %get-tuple-element.197), channel_id=1, source_target_pairs={{0,16},{1,17},{2,18},{3,19},{4,20},{5,21},{6,22},{7,23},{8,24},{9,... | collective-permute-start | bytes 147464 | tf_op jit(solution)/shard_map/ppermute | solution.py:20
  5.8 23.3 %collective-permute-start.1 = (bf16[2,6,4,4,1,1,128]{6,3,2,1,0,5,4:T(4,128)(2,1)S(1)}, bf16[2,6,4,4,1,1,128]{6,3,2,1,0,5,4:T(4,128)(2,1)S(1)}, u32[]{:S(2)}, u32[]{:S(2)}) collective-permute-start(bf16[2,6,4,4,1,1,128]{6,3,2,1,0,5,4:T(4,128)(2,1)S(1)} %get-tuple-element.198), channel_id=1, source_target_pairs={{16,0},{17,1},{18,2},{19,3},{20,4},{21,5},{22,6},{23,7},{24,8},{25... | collective-permute-start | bytes 147464 | tf_op jit(solution)/shard_map/ppermute | solution.py:21
  7.1 22.0 %collective-permute-start.2 = (bf16[2,6,4,4,1,1,128]{6,3,2,1,0,5,4:T(4,128)(2,1)S(1)}, bf16[2,6,4,4,1,1,128]{6,3,2,1,0,5,4:T(4,128)(2,1)S(1)}, u32[]{:S(2)}, u32[]{:S(2)}) collective-permute-start(bf16[2,6,4,4,1,1,128]{6,3,2,1,0,5,4:T(4,128)(2,1)S(1)} %get-tuple-element.195), channel_id=1, source_target_pairs={{0,4},{4,8},{8,12},{1,5},{5,9},{9,13},{2,6},{6,10},{10,14},{3,7},{... | collective-permute-start | bytes 147464 | tf_op jit(solution)/shard_map/ppermute | solution.py:20
  8.6 20.5 %collective-permute-start.3 = (bf16[2,6,4,4,1,1,128]{6,3,2,1,0,5,4:T(4,128)(2,1)S(1)}, bf16[2,6,4,4,1,1,128]{6,3,2,1,0,5,4:T(4,128)(2,1)S(1)}, u32[]{:S(2)}, u32[]{:S(2)}) collective-permute-start(bf16[2,6,4,4,1,1,128]{6,3,2,1,0,5,4:T(4,128)(2,1)S(1)} %get-tuple-element.196), channel_id=1, source_target_pairs={{4,0},{8,4},{12,8},{5,1},{9,5},{13,9},{6,2},{10,6},{14,10},{7,3},{... | collective-permute-start | bytes 147464 | tf_op jit(solution)/shard_map/ppermute | solution.py:21
  11.7 10.5 %all-to-all-start = ((bf16[4,4,384]{2,1,0:T(4,128)(2,1)}), bf16[4,4,384]{2,1,0:T(4,128)(2,1)S(1)}, u32[]{:S(2)}, u32[]{:S(2)}) async-start(bf16[4,4,384]{2,1,0:T(4,128)(2,1)} %copy.260), calls=%async_computation | async-start | bytes 24576 | tf_op jit(solution)/shard_map/all_to_all | solution.py:155
  31.5 10.2 %collective-permute-start.4 = (bf16[2,6,4,4,1,1,128]{6,3,2,1,0,5,4:T(4,128)(2,1)S(1)}, bf16[2,6,4,4,1,1,128]{6,3,2,1,0,5,4:T(4,128)(2,1)S(1)}, u32[]{:S(2)}, u32[]{:S(2)}) collective-permute-start(bf16[2,6,4,4,1,1,128]{6,3,2,1,0,5,4:T(4,128)(2,1)S(1)} %get-tuple-element.187), channel_id=1, source_target_pairs={{0,16},{1,17},{2,18},{3,19},{4,20},{5,21},{6,22},{7,23},{8,24},{9,... | collective-permute-start | bytes 147464 | tf_op jit(solution)/shard_map/ppermute | solution.py:20
  35.9 6.3 %collective-permute-start.5 = (bf16[2,6,4,4,1,1,128]{6,3,2,1,0,5,4:T(4,128)(2,1)S(1)}, bf16[2,6,4,4,1,1,128]{6,3,2,1,0,5,4:T(4,128)(2,1)S(1)}, u32[]{:S(2)}, u32[]{:S(2)}) collective-permute-start(bf16[2,6,4,4,1,1,128]{6,3,2,1,0,5,4:T(4,128)(2,1)S(1)} %get-tuple-element.188), channel_id=1, source_target_pairs={{16,0},{17,1},{18,2},{19,3},{20,4},{21,5},{22,6},{23,7},{24,8},{25... | collective-permute-start | bytes 147464 | tf_op jit(solution)/shard_map/ppermute | solution.py:21
  40.3 6.1 %collective-permute-start.7 = (bf16[2,6,4,4,1,1,128]{6,3,2,1,0,5,4:T(4,128)(2,1)S(1)}, bf16[2,6,4,4,1,1,128]{6,3,2,1,0,5,4:T(4,128)(2,1)S(1)}, u32[]{:S(2)}, u32[]{:S(2)}) collective-permute-start(bf16[2,6,4,4,1,1,128]{6,3,2,1,0,5,4:T(4,128)(2,1)S(1)} %get-tuple-element.186), channel_id=1, source_target_pairs={{4,0},{8,4},{12,8},{5,1},{9,5},{13,9},{6,2},{10,6},{14,10},{7,3},{... | collective-permute-start | bytes 147464 | tf_op jit(solution)/shard_map/ppermute | solution.py:21
  48.7 12.0 %collective-permute-start.10 = (bf16[2,6,4,4,1,1,128]{6,3,2,1,0,5,4:T(4,128)(2,1)S(1)}, bf16[2,6,4,4,1,1,128]{6,3,2,1,0,5,4:T(4,128)(2,1)S(1)}, u32[]{:S(2)}, u32[]{:S(2)}) collective-permute-start(bf16[2,6,4,4,1,1,128]{6,3,2,1,0,5,4:T(4,128)(2,1)S(1)} %get-tuple-element.175), channel_id=1, source_target_pairs={{0,4},{4,8},{8,12},{1,5},{5,9},{9,13},{2,6},{6,10},{10,14},{3,7},{... | collective-permute-start | bytes 147464 | tf_op jit(solution)/shard_map/ppermute | solution.py:20
  53.4 7.3 %collective-permute-start.11 = (bf16[2,6,4,4,1,1,128]{6,3,2,1,0,5,4:T(4,128)(2,1)S(1)}, bf16[2,6,4,4,1,1,128]{6,3,2,1,0,5,4:T(4,128)(2,1)S(1)}, u32[]{:S(2)}, u32[]{:S(2)}) collective-permute-start(bf16[2,6,4,4,1,1,128]{6,3,2,1,0,5,4:T(4,128)(2,1)S(1)} %get-tuple-element.176), channel_id=1, source_target_pairs={{4,0},{8,4},{12,8},{5,1},{9,5},{13,9},{6,2},{10,6},{14,10},{7,3},{... | collective-permute-start | bytes 147464 | tf_op jit(solution)/shard_map/ppermute | solution.py:21
  54.7 6.5 %collective-permute-start.8 = (bf16[2,6,4,4,1,1,128]{6,3,2,1,0,5,4:T(4,128)(2,1)S(1)}, bf16[2,6,4,4,1,1,128]{6,3,2,1,0,5,4:T(4,128)(2,1)S(1)}, u32[]{:S(2)}, u32[]{:S(2)}) collective-permute-start(bf16[2,6,4,4,1,1,128]{6,3,2,1,0,5,4:T(4,128)(2,1)S(1)} %get-tuple-element.177), channel_id=1, source_target_pairs={{0,16},{1,17},{2,18},{3,19},{4,20},{5,21},{6,22},{7,23},{8,24},{9,... | collective-permute-start | bytes 147464 | tf_op jit(solution)/shard_map/ppermute | solution.py:20
  59.3 6.4 %collective-permute-start.9 = (bf16[2,6,4,4,1,1,128]{6,3,2,1,0,5,4:T(4,128)(2,1)S(1)}, bf16[2,6,4,4,1,1,128]{6,3,2,1,0,5,4:T(4,128)(2,1)S(1)}, u32[]{:S(2)}, u32[]{:S(2)}) collective-permute-start(bf16[2,6,4,4,1,1,128]{6,3,2,1,0,5,4:T(4,128)(2,1)S(1)} %get-tuple-element.178), channel_id=1, source_target_pairs={{16,0},{17,1},{18,2},{19,3},{20,4},{21,5},{22,6},{23,7},{24,8},{25... | collective-permute-start | bytes 147464 | tf_op jit(solution)/shard_map/ppermute | solution.py:21
  71.2 51.5 %collective-permute-start.12 = (bf16[2,6,4,4,1,1,128]{6,3,2,1,0,5,4:T(4,128)(2,1)}, bf16[2,6,4,4,1,1,128]{6,3,2,1,0,5,4:T(4,128)(2,1)}, u32[]{:S(2)}, u32[]{:S(2)}) collective-permute-start(bf16[2,6,4,4,1,1,128]{6,3,2,1,0,5,4:T(4,128)(2,1)} %get-tuple-element.167), channel_id=1, source_target_pairs={{0,16},{1,17},{2,18},{3,19},{4,20},{5,21},{6,22},{7,23},{8,24},{9,... | collective-permute-start | bytes 147464 | tf_op jit(solution)/shard_map/ppermute | solution.py:20
  103.2 10.7 %all-to-all-start.1 = ((f32[1,16,384]{2,0,1:T(1,128)}), f32[1,16,384]{2,0,1:T(1,128)}, u32[]{:S(2)}, u32[]{:S(2)}) async-start(f32[1,16,384]{2,0,1:T(1,128)} %psum.14), calls=%async_computation.1 | async-start | bytes 49152 | tf_op jit(solution)/shard_map/all_to_all | solution.py:184
  110.0 12.7 %collective-permute-start.13 = (bf16[2,6,4,4,1,1,128]{6,3,2,1,0,5,4:T(4,128)(2,1)}, bf16[2,6,4,4,1,1,128]{6,3,2,1,0,5,4:T(4,128)(2,1)S(1)}, u32[]{:S(2)}, u32[]{:S(2)}) collective-permute-start(bf16[2,6,4,4,1,1,128]{6,3,2,1,0,5,4:T(4,128)(2,1)} %get-tuple-element.168), channel_id=1, source_target_pairs={{16,0},{17,1},{18,2},{19,3},{20,4},{21,5},{22,6},{23,7},{24,8},{25... | collective-permute-start | bytes 147464 | tf_op jit(solution)/shard_map/ppermute | solution.py:21
  111.3 11.4 %collective-permute-start.14 = (bf16[2,6,4,4,1,1,128]{6,3,2,1,0,5,4:T(4,128)(2,1)}, bf16[2,6,4,4,1,1,128]{6,3,2,1,0,5,4:T(4,128)(2,1)S(1)}, u32[]{:S(2)}, u32[]{:S(2)}) collective-permute-start(bf16[2,6,4,4,1,1,128]{6,3,2,1,0,5,4:T(4,128)(2,1)} %get-tuple-element.165), channel_id=1, source_target_pairs={{0,4},{4,8},{8,12},{1,5},{5,9},{9,13},{2,6},{6,10},{10,14},{3,7},{... | collective-permute-start | bytes 147464 | tf_op jit(solution)/shard_map/ppermute | solution.py:20
  112.6 10.1 %collective-permute-start.15 = (bf16[2,6,4,4,1,1,128]{6,3,2,1,0,5,4:T(4,128)(2,1)}, bf16[2,6,4,4,1,1,128]{6,3,2,1,0,5,4:T(4,128)(2,1)S(1)}, u32[]{:S(2)}, u32[]{:S(2)}) collective-permute-start(bf16[2,6,4,4,1,1,128]{6,3,2,1,0,5,4:T(4,128)(2,1)} %get-tuple-element.166), channel_id=1, source_target_pairs={{4,0},{8,4},{12,8},{5,1},{9,5},{13,9},{6,2},{10,6},{14,10},{7,3},{... | collective-permute-start | bytes 147464 | tf_op jit(solution)/shard_map/ppermute | solution.py:21
  117.6 10.7 %all-to-all-start.2 = ((bf16[4,4,384]{2,1,0:T(4,128)(2,1)}), bf16[4,4,384]{2,1,0:T(4,128)(2,1)S(1)}, u32[]{:S(2)}, u32[]{:S(2)}) async-start(bf16[4,4,384]{2,1,0:T(4,128)(2,1)} %copy.301), calls=%async_computation.2 | async-start | bytes 24576 | tf_op jit(solution)/shard_map/all_to_all | solution.py:155
  137.1 8.6 %collective-permute-start.16 = (bf16[2,6,4,4,1,1,128]{6,3,2,1,0,5,4:T(4,128)(2,1)S(1)}, bf16[2,6,4,4,1,1,128]{6,3,2,1,0,5,4:T(4,128)(2,1)S(1)}, u32[]{:S(2)}, u32[]{:S(2)}) collective-permute-start(bf16[2,6,4,4,1,1,128]{6,3,2,1,0,5,4:T(4,128)(2,1)S(1)} %get-tuple-element.157), channel_id=1, source_target_pairs={{0,16},{1,17},{2,18},{3,19},{4,20},{5,21},{6,22},{7,23},{8,24},{9,... | collective-permute-start | bytes 147464 | tf_op jit(solution)/shard_map/ppermute | solution.py:20
  141.7 6.0 %collective-permute-start.17 = (bf16[2,6,4,4,1,1,128]{6,3,2,1,0,5,4:T(4,128)(2,1)S(1)}, bf16[2,6,4,4,1,1,128]{6,3,2,1,0,5,4:T(4,128)(2,1)S(1)}, u32[]{:S(2)}, u32[]{:S(2)}) collective-permute-start(bf16[2,6,4,4,1,1,128]{6,3,2,1,0,5,4:T(4,128)(2,1)S(1)} %get-tuple-element.158), channel_id=1, source_target_pairs={{16,0},{17,1},{18,2},{19,3},{20,4},{21,5},{22,6},{23,7},{24,8},{25... | collective-permute-start | bytes 147464 | tf_op jit(solution)/shard_map/ppermute | solution.py:21
  144.3 5.3 %collective-permute-start.19 = (bf16[2,6,4,4,1,1,128]{6,3,2,1,0,5,4:T(4,128)(2,1)S(1)}, bf16[2,6,4,4,1,1,128]{6,3,2,1,0,5,4:T(4,128)(2,1)S(1)}, u32[]{:S(2)}, u32[]{:S(2)}) collective-permute-start(bf16[2,6,4,4,1,1,128]{6,3,2,1,0,5,4:T(4,128)(2,1)S(1)} %get-tuple-element.156), channel_id=1, source_target_pairs={{4,0},{8,4},{12,8},{5,1},{9,5},{13,9},{6,2},{10,6},{14,10},{7,3},{... | collective-permute-start | bytes 147464 | tf_op jit(solution)/shard_map/ppermute | solution.py:21
  151.2 12.3 %collective-permute-start.20 = (bf16[2,6,4,4,1,1,128]{6,3,2,1,0,5,4:T(4,128)(2,1)S(1)}, bf16[2,6,4,4,1,1,128]{6,3,2,1,0,5,4:T(4,128)(2,1)S(1)}, u32[]{:S(2)}, u32[]{:S(2)}) collective-permute-start(bf16[2,6,4,4,1,1,128]{6,3,2,1,0,5,4:T(4,128)(2,1)S(1)} %get-tuple-element.147), channel_id=1, source_target_pairs={{0,16},{1,17},{2,18},{3,19},{4,20},{5,21},{6,22},{7,23},{8,24},{9,... | collective-permute-start | bytes 147464 | tf_op jit(solution)/shard_map/ppermute | solution.py:20
  155.7 7.8 %collective-permute-start.21 = (bf16[2,6,4,4,1,1,128]{6,3,2,1,0,5,4:T(4,128)(2,1)S(1)}, bf16[2,6,4,4,1,1,128]{6,3,2,1,0,5,4:T(4,128)(2,1)S(1)}, u32[]{:S(2)}, u32[]{:S(2)}) collective-permute-start(bf16[2,6,4,4,1,1,128]{6,3,2,1,0,5,4:T(4,128)(2,1)S(1)} %get-tuple-element.148), channel_id=1, source_target_pairs={{16,0},{17,1},{18,2},{19,3},{20,4},{21,5},{22,6},{23,7},{24,8},{25... | collective-permute-start | bytes 147464 | tf_op jit(solution)/shard_map/ppermute | solution.py:21
  157.0 6.5 %collective-permute-start.22 = (bf16[2,6,4,4,1,1,128]{6,3,2,1,0,5,4:T(4,128)(2,1)S(1)}, bf16[2,6,4,4,1,1,128]{6,3,2,1,0,5,4:T(4,128)(2,1)S(1)}, u32[]{:S(2)}, u32[]{:S(2)}) collective-permute-start(bf16[2,6,4,4,1,1,128]{6,3,2,1,0,5,4:T(4,128)(2,1)S(1)} %get-tuple-element.145), channel_id=1, source_target_pairs={{0,4},{4,8},{8,12},{1,5},{5,9},{9,13},{2,6},{6,10},{10,14},{3,7},{... | collective-permute-start | bytes 147464 | tf_op jit(solution)/shard_map/ppermute | solution.py:20
  (23 other events, 222.4 us)
where the time goes:
time: 209 us; the launch traced here: 208 us
  starting transfers between devices  70.7 us (34%)
  blocking collectives  56.4 us (27%)
  other arithmetic  28.5 us (14%)
  local copies, waits for them, and re-layouts  21.8 us (10%)
  waiting for transfers between devices  20 us (10%)
  matrix products  7.17 us (3%)
  between operations  2.87 us (1%)
    psum x2, blocking collectives, body(): summed = lax.psum(partial_loads, ('fx', 'fy'))  48.4 us
    ppermute x12, starting transfers between devices, with_halo(): before = lax.ppermute(last, axis, up)  41.3 us
    ppermute x12, starting transfers between devices, with_halo(): after = lax.ppermute(initial, axis, down)  15.5 us
    ppermute x12, waiting for transfers between devices, with_halo(): after = lax.ppermute(initial, axis, down)  13.9 us
    gather x2, local copies, waits for them, and re-layouts, body(): picked = received.reshape(-1)[columns]  10 us
    all_to_all x2, starting transfers between devices, body(): lax.all_to_all(shell_tangent.astype(jnp.bfloat16), 'st', split_axis=0, co...  9.96 us
    scatter-add x2, other arithmetic, body(): jnp.zeros((panels * SDOF * PN,), jnp.float32).at[columns].add(loads)  9.5 us
    all_to_all x1, blocking collectives, body(): lax.all_to_all(summed, 'st', split_axis=1, concat_axis=0, tiled=True)  7.97 us
  transfers between devices with their start and end apart: 27, of which 9 were waited for; matrix products, arithmetic and copies ran while one was open for 13% of the time, Pallas kernels for 0%

commit v1 on v0

--- a/solution.py
+++ b/solution.py
@@ -1,3 +1,4 @@
+import functools
 import jax
 import jax.numpy as jnp
 from jax import lax
@@ -8,6 +9,14 @@
 FSWEEP = 3
 ROUNDS = 2
 SIGMA = 0.5
+
+
+def hold_ratios(view, chip_axis):
+    z = jnp.sum(lax.all_gather(view, chip_axis), axis=0)
+    return z
+
+
+keep_up_object_over_axis = functools.partial(hold_ratios, chip_axis=("fx", "fy"))
 
 
 def with_halo(value, sides, width):
@@ -180,7 +189,7 @@
         panels = received.shape[1]
         partial_loads = jnp.zeros((panels * SDOF * PN,), jnp.float32).at[columns].add(loads)
         partial_loads = partial_loads.reshape(1, panels, SDOF * PN)
-        summed = lax.psum(partial_loads, ("fx", "fy"))
+        summed = keep_up_object_over_axis(partial_loads)
         owned = lax.all_to_all(summed, "st", split_axis=1, concat_axis=0, tiled=True)
         shell_adjoint = shell_solve(shell_adjoint_rhs - owned)
         shell_tangent = shell_solve(shell_load + shell_adjoint)

time: 209 us -> 181 us (0.87)
  blocking collectives: 56.4 us -> 28.9 us
    psum x2 -> x0, blocking collectives: 48.4 us -> none  [body(): summed = lax.psum(partial_loads, ('fx', 'fy'))]
    all_gather x0 -> x2, blocking collectives: none -> 20.9 us  [hold_ratios(): z = jnp.sum(lax.all_gather(view, chip_axis), axis=0)]
  transfers between devices with their start and end apart: 27 -> 27, of which waited for: 9 -> 9; matrix products, arithmetic and copies ran while one was open for 13% -> 14% of each run, Pallas kernels for 0% -> 0%
where the time goes in v1:
time: 181 us; the launch traced here: 180 us
  starting transfers between devices  71 us (39%)
  blocking collectives  28.9 us (16%)
  other arithmetic  26.9 us (15%)
  local copies, waits for them, and re-layouts  22.1 us (12%)
  waiting for transfers between devices  21.2 us (12%)
  matrix products  6.55 us (4%)
  between operations  2.98 us (2%)
    ppermute x12, starting transfers between devices, with_halo(): before = lax.ppermute(last, axis, up)  42 us
    all_gather x2, blocking collectives, hold_ratios(): z = jnp.sum(lax.all_gather(view, chip_axis), axis=0)  20.9 us
    ppermute x12, starting transfers between devices, with_halo(): after = lax.ppermute(initial, axis, down)  15.5 us
    ppermute x12, waiting for transfers between devices, with_halo(): after = lax.ppermute(initial, axis, down)  14.6 us
    gather x2, local copies, waits for them, and re-layouts, body(): picked = received.reshape(-1)[columns]  10 us
    all_to_all x2, starting transfers between devices, body(): lax.all_to_all(shell_tangent.astype(jnp.bfloat16), 'st', split_axis=0, co...  9.62 us
    scatter-add x2, other arithmetic, body(): jnp.zeros((panels * SDOF * PN,), jnp.float32).at[columns].add(loads)  9.5 us
    all_to_all x1, blocking collectives, body(): lax.all_to_all(summed, 'st', split_axis=1, concat_axis=0, tiled=True)  7.99 us
  transfers between devices with their start and end apart: 27, of which 9 were waited for; matrix products, arithmetic and copies ran while one was open for 14% of the time, Pallas kernels for 0%

profile of v1, /device:TPU:0, one launch (start us, length us, event | category | flops | bytes accessed | tf_op | source)
XLA Modules:
  0.0 179.7 jit_solution(4400535876023862956)
XLA Ops:
  0.7 5.0 %collective-permute-start = (bf16[2,6,4,4,1,1,128]{6,3,2,1,0,5,4:T(4,128)(2,1)S(1)}, bf16[2,6,4,4,1,1,128]{6,3,2,1,0,5,4:T(4,128)(2,1)S(1)}, u32[]{:S(2)}, u32[]{:S(2)}) collective-permute-start(bf16[2,6,4,4,1,1,128]{6,3,2,1,0,5,4:T(4,128)(2,1)S(1)} %get-tuple-element.197), channel_id=1, source_target_pairs={{0,16},{1,17},{2,18},{3,19},{4,20},{5,21},{6,22},{7,23},{8,24},{9,... | collective-permute-start | bytes 147464 | tf_op jit(solution)/shard_map/ppermute | solution.py:29
  11.7 4.9 %all-to-all-start = ((bf16[4,4,384]{2,1,0:T(4,128)(2,1)}), bf16[4,4,384]{2,1,0:T(4,128)(2,1)S(1)}, u32[]{:S(2)}, u32[]{:S(2)}) async-start(bf16[4,4,384]{2,1,0:T(4,128)(2,1)} %copy.260), calls=%async_computation | async-start | bytes 24576 | tf_op jit(solution)/shard_map/all_to_all | solution.py:164
  22.2 5.0 %gather_fusion = bf16[768]{0:T(1024)(128)(2,1)S(1)} fusion(bf16[6144]{0:T(1024)(128)(2,1)S(1)} %reshape.2595, s32[1024]{0:T(1024)S(1)} %pad_clamp_fusion.1), kind=kCustom, calls=%fused_computation | custom fusion | bytes 6144 | tf_op jit(solution)/shard_map/gather | solution.py:167
  31.5 4.4 %collective-permute-start.4 = (bf16[2,6,4,4,1,1,128]{6,3,2,1,0,5,4:T(4,128)(2,1)S(1)}, bf16[2,6,4,4,1,1,128]{6,3,2,1,0,5,4:T(4,128)(2,1)S(1)}, u32[]{:S(2)}, u32[]{:S(2)}) collective-permute-start(bf16[2,6,4,4,1,1,128]{6,3,2,1,0,5,4:T(4,128)(2,1)S(1)} %get-tuple-element.187), channel_id=1, source_target_pairs={{0,16},{1,17},{2,18},{3,19},{4,20},{5,21},{6,22},{7,23},{8,24},{9,... | collective-permute-start | bytes 147464 | tf_op jit(solution)/shard_map/ppermute | solution.py:29
  37.2 3.0 %collective-permute-start.6 = (bf16[2,6,4,4,1,1,128]{6,3,2,1,0,5,4:T(4,128)(2,1)S(1)}, bf16[2,6,4,4,1,1,128]{6,3,2,1,0,5,4:T(4,128)(2,1)S(1)}, u32[]{:S(2)}, u32[]{:S(2)}) collective-permute-start(bf16[2,6,4,4,1,1,128]{6,3,2,1,0,5,4:T(4,128)(2,1)S(1)} %get-tuple-element.185), channel_id=1, source_target_pairs={{0,4},{4,8},{8,12},{1,5},{5,9},{9,13},{2,6},{6,10},{10,14},{3,7},{... | collective-permute-start | bytes 147464 | tf_op jit(solution)/shard_map/ppermute | solution.py:29
  42.3 4.1 %collective-permute-done.7 = bf16[2,6,4,4,1,1,128]{6,3,2,1,0,5,4:T(4,128)(2,1)S(1)} collective-permute-done((bf16[2,6,4,4,1,1,128]{6,3,2,1,0,5,4:T(4,128)(2,1)S(1)}, bf16[2,6,4,4,1,1,128]{6,3,2,1,0,5,4:T(4,128)(2,1)S(1)}, u32[]{:S(2)}, u32[]{:S(2)}) %collective-permute-start.7) | collective-permute-done | bytes 49184 | tf_op jit(solution)/shard_map/ppermute | solution.py:30
  48.7 4.7 %collective-permute-start.10 = (bf16[2,6,4,4,1,1,128]{6,3,2,1,0,5,4:T(4,128)(2,1)S(1)}, bf16[2,6,4,4,1,1,128]{6,3,2,1,0,5,4:T(4,128)(2,1)S(1)}, u32[]{:S(2)}, u32[]{:S(2)}) collective-permute-start(bf16[2,6,4,4,1,1,128]{6,3,2,1,0,5,4:T(4,128)(2,1)S(1)} %get-tuple-element.175), channel_id=1, source_target_pairs={{0,4},{4,8},{8,12},{1,5},{5,9},{9,13},{2,6},{6,10},{10,14},{3,7},{... | collective-permute-start | bytes 147464 | tf_op jit(solution)/shard_map/ppermute | solution.py:29
  54.7 4.5 %collective-permute-start.8 = (bf16[2,6,4,4,1,1,128]{6,3,2,1,0,5,4:T(4,128)(2,1)S(1)}, bf16[2,6,4,4,1,1,128]{6,3,2,1,0,5,4:T(4,128)(2,1)S(1)}, u32[]{:S(2)}, u32[]{:S(2)}) collective-permute-start(bf16[2,6,4,4,1,1,128]{6,3,2,1,0,5,4:T(4,128)(2,1)S(1)} %get-tuple-element.177), channel_id=1, source_target_pairs={{0,16},{1,17},{2,18},{3,19},{4,20},{5,21},{6,22},{7,23},{8,24},{9,... | collective-permute-start | bytes 147464 | tf_op jit(solution)/shard_map/ppermute | solution.py:29
  61.2 4.4 %collective-permute-done.9 = bf16[2,6,4,4,1,1,128]{6,3,2,1,0,5,4:T(4,128)(2,1)S(1)} collective-permute-done((bf16[2,6,4,4,1,1,128]{6,3,2,1,0,5,4:T(4,128)(2,1)S(1)}, bf16[2,6,4,4,1,1,128]{6,3,2,1,0,5,4:T(4,128)(2,1)S(1)}, u32[]{:S(2)}, u32[]{:S(2)}) %collective-permute-start.9) | collective-permute-done | bytes 49184 | tf_op jit(solution)/shard_map/ppermute | solution.py:30
  71.8 2.1 %collective-permute-start.12 = (bf16[2,6,4,4,1,1,128]{6,3,2,1,0,5,4:T(4,128)(2,1)}, bf16[2,6,4,4,1,1,128]{6,3,2,1,0,5,4:T(4,128)(2,1)}, u32[]{:S(2)}, u32[]{:S(2)}) collective-permute-start(bf16[2,6,4,4,1,1,128]{6,3,2,1,0,5,4:T(4,128)(2,1)} %get-tuple-element.167), channel_id=1, source_target_pairs={{0,16},{1,17},{2,18},{3,19},{4,20},{5,21},{6,22},{7,23},{8,24},{9,... | collective-permute-start | bytes 147464 | tf_op jit(solution)/shard_map/ppermute | solution.py:29
  75.0 4.8 %scatter_custom_fusion.1 = f32[6144]{0:T(1024)S(1)} fusion(s32[768]{0:T(1024)} %copy-done.16, f32[768]{0:T(1024)S(1)} %fusion.5, f32[]{:T(128)} %constant.129.clone.1), kind=kCustom, calls=%fused_computation.296 | custom fusion | flops 768 | bytes 25088 | tf_op jit(solution)/shard_map/scatter-add | solution.py:190
  79.8 9.9 %all_gather.6 = f32[8,1,16,384]{3,2,1,0:T(8,128)S(1)} all-gather(f32[1,1,16,384]{3,2,1,0:T(8,128)S(1)} %all_gather_reshape.6), channel_id=1, replica_groups=mesh['fx'=2,'fy'=4,'st'=4] {'fx','fy'}, dimensions={0}, use_global_device_ids=true | all-gather | bytes 221184 | tf_op jit(solution)/shard_map/all_gather | solution.py:15
  90.4 3.9 %all-to-all-start.1 = ((f32[1,16,384]{2,0,1:T(1,128)}), f32[1,16,384]{2,0,1:T(1,128)}, u32[]{:S(2)}, u32[]{:S(2)}) async-start(f32[1,16,384]{2,0,1:T(1,128)} %reduce_sum.365), calls=%async_computation.1 | async-start | bytes 49152 | tf_op jit(solution)/shard_map/all_to_all | solution.py:193
  96.7 2.3 %collective-permute-start.14 = (bf16[2,6,4,4,1,1,128]{6,3,2,1,0,5,4:T(4,128)(2,1)}, bf16[2,6,4,4,1,1,128]{6,3,2,1,0,5,4:T(4,128)(2,1)S(1)}, u32[]{:S(2)}, u32[]{:S(2)}) collective-permute-start(bf16[2,6,4,4,1,1,128]{6,3,2,1,0,5,4:T(4,128)(2,1)} %get-tuple-element.165), channel_id=1, source_target_pairs={{0,4},{4,8},{8,12},{1,5},{5,9},{9,13},{2,6},{6,10},{10,14},{3,7},{... | collective-permute-start | bytes 147464 | tf_op jit(solution)/shard_map/ppermute | solution.py:29
  104.0 4.7 %all-to-all-start.2 = ((bf16[4,4,384]{2,1,0:T(4,128)(2,1)}), bf16[4,4,384]{2,1,0:T(4,128)(2,1)S(1)}, u32[]{:S(2)}, u32[]{:S(2)}) async-start(bf16[4,4,384]{2,1,0:T(4,128)(2,1)} %copy.301), calls=%async_computation.2 | async-start | bytes 24576 | tf_op jit(solution)/shard_map/all_to_all | solution.py:164
  110.0 4.4 %all-to-all-done.2 = bf16[4,4,384]{2,1,0:T(4,128)(2,1)S(1)} async-done(((bf16[4,4,384]{2,1,0:T(4,128)(2,1)}), bf16[4,4,384]{2,1,0:T(4,128)(2,1)S(1)}, u32[]{:S(2)}, u32[]{:S(2)}) %all-to-all-start.2) | async-done | bytes 12320 | tf_op jit(solution)/shard_map/all_to_all | solution.py:164
  114.4 5.0 %gather_fusion.2 = bf16[768]{0:T(1024)(128)(2,1)S(1)} fusion(bf16[6144]{0:T(1024)(128)(2,1)S(1)} %reshape.2607, s32[1024]{0:T(1024)S(1)} %pad_clamp_fusion.1), kind=kCustom, calls=%fused_computation.2 | custom fusion | bytes 6144 | tf_op jit(solution)/shard_map/gather | solution.py:167
  123.2 4.3 %collective-permute-start.16 = (bf16[2,6,4,4,1,1,128]{6,3,2,1,0,5,4:T(4,128)(2,1)S(1)}, bf16[2,6,4,4,1,1,128]{6,3,2,1,0,5,4:T(4,128)(2,1)S(1)}, u32[]{:S(2)}, u32[]{:S(2)}) collective-permute-start(bf16[2,6,4,4,1,1,128]{6,3,2,1,0,5,4:T(4,128)(2,1)S(1)} %get-tuple-element.157), channel_id=1, source_target_pairs={{0,16},{1,17},{2,18},{3,19},{4,20},{5,21},{6,22},{7,23},{8,24},{9,... | collective-permute-start | bytes 147464 | tf_op jit(solution)/shard_map/ppermute | solution.py:29
  133.5 2.6 %collective-permute-done.19 = bf16[2,6,4,4,1,1,128]{6,3,2,1,0,5,4:T(4,128)(2,1)S(1)} collective-permute-done((bf16[2,6,4,4,1,1,128]{6,3,2,1,0,5,4:T(4,128)(2,1)S(1)}, bf16[2,6,4,4,1,1,128]{6,3,2,1,0,5,4:T(4,128)(2,1)S(1)}, u32[]{:S(2)}, u32[]{:S(2)}) %collective-permute-start.19) | collective-permute-done | bytes 49184 | tf_op jit(solution)/shard_map/ppermute | solution.py:30
  137.7 4.5 %collective-permute-start.20 = (bf16[2,6,4,4,1,1,128]{6,3,2,1,0,5,4:T(4,128)(2,1)S(1)}, bf16[2,6,4,4,1,1,128]{6,3,2,1,0,5,4:T(4,128)(2,1)S(1)}, u32[]{:S(2)}, u32[]{:S(2)}) collective-permute-start(bf16[2,6,4,4,1,1,128]{6,3,2,1,0,5,4:T(4,128)(2,1)S(1)} %get-tuple-element.147), channel_id=1, source_target_pairs={{0,16},{1,17},{2,18},{3,19},{4,20},{5,21},{6,22},{7,23},{8,24},{9,... | collective-permute-start | bytes 147464 | tf_op jit(solution)/shard_map/ppermute | solution.py:29
  143.5 4.4 %collective-permute-start.22 = (bf16[2,6,4,4,1,1,128]{6,3,2,1,0,5,4:T(4,128)(2,1)S(1)}, bf16[2,6,4,4,1,1,128]{6,3,2,1,0,5,4:T(4,128)(2,1)S(1)}, u32[]{:S(2)}, u32[]{:S(2)}) collective-permute-start(bf16[2,6,4,4,1,1,128]{6,3,2,1,0,5,4:T(4,128)(2,1)S(1)} %get-tuple-element.145), channel_id=1, source_target_pairs={{0,4},{4,8},{8,12},{1,5},{5,9},{9,13},{2,6},{6,10},{10,14},{3,7},{... | collective-permute-start | bytes 147464 | tf_op jit(solution)/shard_map/ppermute | solution.py:29
  153.6 4.8 %scatter_custom_fusion.3 = f32[6144]{0:T(1024)S(1)} fusion(s32[768]{0:T(1024)} %copy-done.16, f32[768]{0:T(1024)S(1)} %fusion.4, f32[]{:T(128)} %constant.129.clone.1), kind=kCustom, calls=%fused_computation.294 | custom fusion | flops 768 | bytes 25088 | tf_op jit(solution)/shard_map/scatter-add | solution.py:190
  158.4 11.0 %all_gather.7 = f32[8,1,16,384]{3,2,1,0:T(8,128)S(1)} all-gather(f32[1,1,16,384]{3,2,1,0:T(8,128)S(1)} %all_gather_reshape.7), channel_id=1, replica_groups=mesh['fx'=2,'fy'=4,'st'=4] {'fx','fy'}, dimensions={0}, use_global_device_ids=true | all-gather | bytes 221184 | tf_op jit(solution)/shard_map/all_gather | solution.py:15
  169.4 8.0 %all_to_all.42 = f32[1,16,384]{2,0,1:T(1,128)S(1)} all-to-all(f32[1,16,384]{2,0,1:T(1,128)S(1)} %reduce_sum.385), channel_id=1, replica_groups=mesh['fx'=2,'fy'=4,'st'=4] {'st'}, dimensions={1} | all-to-all | bytes 49152 | tf_op jit(solution)/shard_map/all_to_all | solution.py:193
  (282 shorter events, 60.1 us)
Async XLA Ops:
  0.7 28.4 %collective-permute-start = (bf16[2,6,4,4,1,1,128]{6,3,2,1,0,5,4:T(4,128)(2,1)S(1)}, bf16[2,6,4,4,1,1,128]{6,3,2,1,0,5,4:T(4,128)(2,1)S(1)}, u32[]{:S(2)}, u32[]{:S(2)}) collective-permute-start(bf16[2,6,4,4,1,1,128]{6,3,2,1,0,5,4:T(4,128)(2,1)S(1)} %get-tuple-element.197), channel_id=1, source_target_pairs={{0,16},{1,17},{2,18},{3,19},{4,20},{5,21},{6,22},{7,23},{8,24},{9,... | collective-permute-start | bytes 147464 | tf_op jit(solution)/shard_map/ppermute | solution.py:29
  5.8 23.3 %collective-permute-start.1 = (bf16[2,6,4,4,1,1,128]{6,3,2,1,0,5,4:T(4,128)(2,1)S(1)}, bf16[2,6,4,4,1,1,128]{6,3,2,1,0,5,4:T(4,128)(2,1)S(1)}, u32[]{:S(2)}, u32[]{:S(2)}) collective-permute-start(bf16[2,6,4,4,1,1,128]{6,3,2,1,0,5,4:T(4,128)(2,1)S(1)} %get-tuple-element.198), channel_id=1, source_target_pairs={{16,0},{17,1},{18,2},{19,3},{20,4},{21,5},{22,6},{23,7},{24,8},{25... | collective-permute-start | bytes 147464 | tf_op jit(solution)/shard_map/ppermute | solution.py:30
  7.1 22.0 %collective-permute-start.2 = (bf16[2,6,4,4,1,1,128]{6,3,2,1,0,5,4:T(4,128)(2,1)S(1)}, bf16[2,6,4,4,1,1,128]{6,3,2,1,0,5,4:T(4,128)(2,1)S(1)}, u32[]{:S(2)}, u32[]{:S(2)}) collective-permute-start(bf16[2,6,4,4,1,1,128]{6,3,2,1,0,5,4:T(4,128)(2,1)S(1)} %get-tuple-element.195), channel_id=1, source_target_pairs={{0,4},{4,8},{8,12},{1,5},{5,9},{9,13},{2,6},{6,10},{10,14},{3,7},{... | collective-permute-start | bytes 147464 | tf_op jit(solution)/shard_map/ppermute | solution.py:29
  8.6 20.5 %collective-permute-start.3 = (bf16[2,6,4,4,1,1,128]{6,3,2,1,0,5,4:T(4,128)(2,1)S(1)}, bf16[2,6,4,4,1,1,128]{6,3,2,1,0,5,4:T(4,128)(2,1)S(1)}, u32[]{:S(2)}, u32[]{:S(2)}) collective-permute-start(bf16[2,6,4,4,1,1,128]{6,3,2,1,0,5,4:T(4,128)(2,1)S(1)} %get-tuple-element.196), channel_id=1, source_target_pairs={{4,0},{8,4},{12,8},{5,1},{9,5},{13,9},{6,2},{10,6},{14,10},{7,3},{... | collective-permute-start | bytes 147464 | tf_op jit(solution)/shard_map/ppermute | solution.py:30
  11.7 10.5 %all-to-all-start = ((bf16[4,4,384]{2,1,0:T(4,128)(2,1)}), bf16[4,4,384]{2,1,0:T(4,128)(2,1)S(1)}, u32[]{:S(2)}, u32[]{:S(2)}) async-start(bf16[4,4,384]{2,1,0:T(4,128)(2,1)} %copy.260), calls=%async_computation | async-start | bytes 24576 | tf_op jit(solution)/shard_map/all_to_all | solution.py:164
  31.5 10.2 %collective-permute-start.4 = (bf16[2,6,4,4,1,1,128]{6,3,2,1,0,5,4:T(4,128)(2,1)S(1)}, bf16[2,6,4,4,1,1,128]{6,3,2,1,0,5,4:T(4,128)(2,1)S(1)}, u32[]{:S(2)}, u32[]{:S(2)}) collective-permute-start(bf16[2,6,4,4,1,1,128]{6,3,2,1,0,5,4:T(4,128)(2,1)S(1)} %get-tuple-element.187), channel_id=1, source_target_pairs={{0,16},{1,17},{2,18},{3,19},{4,20},{5,21},{6,22},{7,23},{8,24},{9,... | collective-permute-start | bytes 147464 | tf_op jit(solution)/shard_map/ppermute | solution.py:29
  35.9 6.3 %collective-permute-start.5 = (bf16[2,6,4,4,1,1,128]{6,3,2,1,0,5,4:T(4,128)(2,1)S(1)}, bf16[2,6,4,4,1,1,128]{6,3,2,1,0,5,4:T(4,128)(2,1)S(1)}, u32[]{:S(2)}, u32[]{:S(2)}) collective-permute-start(bf16[2,6,4,4,1,1,128]{6,3,2,1,0,5,4:T(4,128)(2,1)S(1)} %get-tuple-element.188), channel_id=1, source_target_pairs={{16,0},{17,1},{18,2},{19,3},{20,4},{21,5},{22,6},{23,7},{24,8},{25... | collective-permute-start | bytes 147464 | tf_op jit(solution)/shard_map/ppermute | solution.py:30
  40.3 6.1 %collective-permute-start.7 = (bf16[2,6,4,4,1,1,128]{6,3,2,1,0,5,4:T(4,128)(2,1)S(1)}, bf16[2,6,4,4,1,1,128]{6,3,2,1,0,5,4:T(4,128)(2,1)S(1)}, u32[]{:S(2)}, u32[]{:S(2)}) collective-permute-start(bf16[2,6,4,4,1,1,128]{6,3,2,1,0,5,4:T(4,128)(2,1)S(1)} %get-tuple-element.186), channel_id=1, source_target_pairs={{4,0},{8,4},{12,8},{5,1},{9,5},{13,9},{6,2},{10,6},{14,10},{7,3},{... | collective-permute-start | bytes 147464 | tf_op jit(solution)/shard_map/ppermute | solution.py:30
  48.7 12.0 %collective-permute-start.10 = (bf16[2,6,4,4,1,1,128]{6,3,2,1,0,5,4:T(4,128)(2,1)S(1)}, bf16[2,6,4,4,1,1,128]{6,3,2,1,0,5,4:T(4,128)(2,1)S(1)}, u32[]{:S(2)}, u32[]{:S(2)}) collective-permute-start(bf16[2,6,4,4,1,1,128]{6,3,2,1,0,5,4:T(4,128)(2,1)S(1)} %get-tuple-element.175), channel_id=1, source_target_pairs={{0,4},{4,8},{8,12},{1,5},{5,9},{9,13},{2,6},{6,10},{10,14},{3,7},{... | collective-permute-start | bytes 147464 | tf_op jit(solution)/shard_map/ppermute | solution.py:29
  53.4 7.3 %collective-permute-start.11 = (bf16[2,6,4,4,1,1,128]{6,3,2,1,0,5,4:T(4,128)(2,1)S(1)}, bf16[2,6,4,4,1,1,128]{6,3,2,1,0,5,4:T(4,128)(2,1)S(1)}, u32[]{:S(2)}, u32[]{:S(2)}) collective-permute-start(bf16[2,6,4,4,1,1,128]{6,3,2,1,0,5,4:T(4,128)(2,1)S(1)} %get-tuple-element.176), channel_id=1, source_target_pairs={{4,0},{8,4},{12,8},{5,1},{9,5},{13,9},{6,2},{10,6},{14,10},{7,3},{... | collective-permute-start | bytes 147464 | tf_op jit(solution)/shard_map/ppermute | solution.py:30
  54.7 6.5 %collective-permute-start.8 = (bf16[2,6,4,4,1,1,128]{6,3,2,1,0,5,4:T(4,128)(2,1)S(1)}, bf16[2,6,4,4,1,1,128]{6,3,2,1,0,5,4:T(4,128)(2,1)S(1)}, u32[]{:S(2)}, u32[]{:S(2)}) collective-permute-start(bf16[2,6,4,4,1,1,128]{6,3,2,1,0,5,4:T(4,128)(2,1)S(1)} %get-tuple-element.177), channel_id=1, source_target_pairs={{0,16},{1,17},{2,18},{3,19},{4,20},{5,21},{6,22},{7,23},{8,24},{9,... | collective-permute-start | bytes 147464 | tf_op jit(solution)/shard_map/ppermute | solution.py:29
  59.3 6.4 %collective-permute-start.9 = (bf16[2,6,4,4,1,1,128]{6,3,2,1,0,5,4:T(4,128)(2,1)S(1)}, bf16[2,6,4,4,1,1,128]{6,3,2,1,0,5,4:T(4,128)(2,1)S(1)}, u32[]{:S(2)}, u32[]{:S(2)}) collective-permute-start(bf16[2,6,4,4,1,1,128]{6,3,2,1,0,5,4:T(4,128)(2,1)S(1)} %get-tuple-element.178), channel_id=1, source_target_pairs={{16,0},{17,1},{18,2},{19,3},{20,4},{21,5},{22,6},{23,7},{24,8},{25... | collective-permute-start | bytes 147464 | tf_op jit(solution)/shard_map/ppermute | solution.py:30
  71.8 36.9 %collective-permute-start.12 = (bf16[2,6,4,4,1,1,128]{6,3,2,1,0,5,4:T(4,128)(2,1)}, bf16[2,6,4,4,1,1,128]{6,3,2,1,0,5,4:T(4,128)(2,1)}, u32[]{:S(2)}, u32[]{:S(2)}) collective-permute-start(bf16[2,6,4,4,1,1,128]{6,3,2,1,0,5,4:T(4,128)(2,1)} %get-tuple-element.167), channel_id=1, source_target_pairs={{0,16},{1,17},{2,18},{3,19},{4,20},{5,21},{6,22},{7,23},{8,24},{9,... | collective-permute-start | bytes 147464 | tf_op jit(solution)/shard_map/ppermute | solution.py:29
  90.4 9.9 %all-to-all-start.1 = ((f32[1,16,384]{2,0,1:T(1,128)}), f32[1,16,384]{2,0,1:T(1,128)}, u32[]{:S(2)}, u32[]{:S(2)}) async-start(f32[1,16,384]{2,0,1:T(1,128)} %reduce_sum.365), calls=%async_computation.1 | async-start | bytes 49152 | tf_op jit(solution)/shard_map/all_to_all | solution.py:193
  95.4 13.4 %collective-permute-start.13 = (bf16[2,6,4,4,1,1,128]{6,3,2,1,0,5,4:T(4,128)(2,1)}, bf16[2,6,4,4,1,1,128]{6,3,2,1,0,5,4:T(4,128)(2,1)S(1)}, u32[]{:S(2)}, u32[]{:S(2)}) collective-permute-start(bf16[2,6,4,4,1,1,128]{6,3,2,1,0,5,4:T(4,128)(2,1)} %get-tuple-element.168), channel_id=1, source_target_pairs={{16,0},{17,1},{18,2},{19,3},{20,4},{21,5},{22,6},{23,7},{24,8},{25... | collective-permute-start | bytes 147464 | tf_op jit(solution)/shard_map/ppermute | solution.py:30
  96.7 12.1 %collective-permute-start.14 = (bf16[2,6,4,4,1,1,128]{6,3,2,1,0,5,4:T(4,128)(2,1)}, bf16[2,6,4,4,1,1,128]{6,3,2,1,0,5,4:T(4,128)(2,1)S(1)}, u32[]{:S(2)}, u32[]{:S(2)}) collective-permute-start(bf16[2,6,4,4,1,1,128]{6,3,2,1,0,5,4:T(4,128)(2,1)} %get-tuple-element.165), channel_id=1, source_target_pairs={{0,4},{4,8},{8,12},{1,5},{5,9},{9,13},{2,6},{6,10},{10,14},{3,7},{... | collective-permute-start | bytes 147464 | tf_op jit(solution)/shard_map/ppermute | solution.py:29
  98.9 9.8 %collective-permute-start.15 = (bf16[2,6,4,4,1,1,128]{6,3,2,1,0,5,4:T(4,128)(2,1)}, bf16[2,6,4,4,1,1,128]{6,3,2,1,0,5,4:T(4,128)(2,1)S(1)}, u32[]{:S(2)}, u32[]{:S(2)}) collective-permute-start(bf16[2,6,4,4,1,1,128]{6,3,2,1,0,5,4:T(4,128)(2,1)} %get-tuple-element.166), channel_id=1, source_target_pairs={{4,0},{8,4},{12,8},{5,1},{9,5},{13,9},{6,2},{10,6},{14,10},{7,3},{... | collective-permute-start | bytes 147464 | tf_op jit(solution)/shard_map/ppermute | solution.py:30
  104.0 10.3 %all-to-all-start.2 = ((bf16[4,4,384]{2,1,0:T(4,128)(2,1)}), bf16[4,4,384]{2,1,0:T(4,128)(2,1)S(1)}, u32[]{:S(2)}, u32[]{:S(2)}) async-start(bf16[4,4,384]{2,1,0:T(4,128)(2,1)} %copy.301), calls=%async_computation.2 | async-start | bytes 24576 | tf_op jit(solution)/shard_map/all_to_all | solution.py:164
  123.2 8.3 %collective-permute-start.16 = (bf16[2,6,4,4,1,1,128]{6,3,2,1,0,5,4:T(4,128)(2,1)S(1)}, bf16[2,6,4,4,1,1,128]{6,3,2,1,0,5,4:T(4,128)(2,1)S(1)}, u32[]{:S(2)}, u32[]{:S(2)}) collective-permute-start(bf16[2,6,4,4,1,1,128]{6,3,2,1,0,5,4:T(4,128)(2,1)S(1)} %get-tuple-element.157), channel_id=1, source_target_pairs={{0,16},{1,17},{2,18},{3,19},{4,20},{5,21},{6,22},{7,23},{8,24},{9,... | collective-permute-start | bytes 147464 | tf_op jit(solution)/shard_map/ppermute | solution.py:29
  127.5 6.0 %collective-permute-start.17 = (bf16[2,6,4,4,1,1,128]{6,3,2,1,0,5,4:T(4,128)(2,1)S(1)}, bf16[2,6,4,4,1,1,128]{6,3,2,1,0,5,4:T(4,128)(2,1)S(1)}, u32[]{:S(2)}, u32[]{:S(2)}) collective-permute-start(bf16[2,6,4,4,1,1,128]{6,3,2,1,0,5,4:T(4,128)(2,1)S(1)} %get-tuple-element.158), channel_id=1, source_target_pairs={{16,0},{17,1},{18,2},{19,3},{20,4},{21,5},{22,6},{23,7},{24,8},{25... | collective-permute-start | bytes 147464 | tf_op jit(solution)/shard_map/ppermute | solution.py:30
  130.1 5.9 %collective-permute-start.19 = (bf16[2,6,4,4,1,1,128]{6,3,2,1,0,5,4:T(4,128)(2,1)S(1)}, bf16[2,6,4,4,1,1,128]{6,3,2,1,0,5,4:T(4,128)(2,1)S(1)}, u32[]{:S(2)}, u32[]{:S(2)}) collective-permute-start(bf16[2,6,4,4,1,1,128]{6,3,2,1,0,5,4:T(4,128)(2,1)S(1)} %get-tuple-element.156), channel_id=1, source_target_pairs={{4,0},{8,4},{12,8},{5,1},{9,5},{13,9},{6,2},{10,6},{14,10},{7,3},{... | collective-permute-start | bytes 147464 | tf_op jit(solution)/shard_map/ppermute | solution.py:30
  137.7 12.4 %collective-permute-start.20 = (bf16[2,6,4,4,1,1,128]{6,3,2,1,0,5,4:T(4,128)(2,1)S(1)}, bf16[2,6,4,4,1,1,128]{6,3,2,1,0,5,4:T(4,128)(2,1)S(1)}, u32[]{:S(2)}, u32[]{:S(2)}) collective-permute-start(bf16[2,6,4,4,1,1,128]{6,3,2,1,0,5,4:T(4,128)(2,1)S(1)} %get-tuple-element.147), channel_id=1, source_target_pairs={{0,16},{1,17},{2,18},{3,19},{4,20},{5,21},{6,22},{7,23},{8,24},{9,... | collective-permute-start | bytes 147464 | tf_op jit(solution)/shard_map/ppermute | solution.py:29
  142.2 7.8 %collective-permute-start.21 = (bf16[2,6,4,4,1,1,128]{6,3,2,1,0,5,4:T(4,128)(2,1)S(1)}, bf16[2,6,4,4,1,1,128]{6,3,2,1,0,5,4:T(4,128)(2,1)S(1)}, u32[]{:S(2)}, u32[]{:S(2)}) collective-permute-start(bf16[2,6,4,4,1,1,128]{6,3,2,1,0,5,4:T(4,128)(2,1)S(1)} %get-tuple-element.148), channel_id=1, source_target_pairs={{16,0},{17,1},{18,2},{19,3},{20,4},{21,5},{22,6},{23,7},{24,8},{25... | collective-permute-start | bytes 147464 | tf_op jit(solution)/shard_map/ppermute | solution.py:30
  143.5 6.5 %collective-permute-start.22 = (bf16[2,6,4,4,1,1,128]{6,3,2,1,0,5,4:T(4,128)(2,1)S(1)}, bf16[2,6,4,4,1,1,128]{6,3,2,1,0,5,4:T(4,128)(2,1)S(1)}, u32[]{:S(2)}, u32[]{:S(2)}) collective-permute-start(bf16[2,6,4,4,1,1,128]{6,3,2,1,0,5,4:T(4,128)(2,1)S(1)} %get-tuple-element.145), channel_id=1, source_target_pairs={{0,4},{4,8},{8,12},{1,5},{5,9},{9,13},{2,6},{6,10},{10,14},{3,7},{... | collective-permute-start | bytes 147464 | tf_op jit(solution)/shard_map/ppermute | solution.py:29
  (29 other events, 298.7 us)
